TPU v7x, 32 devices: a whole 2x2x4 slice. The times are simulated.
32 devices in a mesh: pipe: 2 (over core), row: 4 (over z), rep: 4 (over y, x).
Axes of the slice: x: 2, y: 2, z: 4, core: 2. Of those that a mesh axis runs over, the one named last changes fastest.
Arguments:
- features: bfloat16 [1, 4096, 256], P(None, ('pipe', 'row')), may hold values from -6 to 6
- tile_src: int32 [8, 4, 2, 12], P(('pipe', 'row'), 'rep'), may hold values from 0 to 7
- tile_dst: int32 [8, 4, 2, 12], P(('pipe', 'row'), 'rep'), may hold values from 0 to 7
- tile_count: int32 [8, 4, 2], P(('pipe', 'row'), 'rep'), may hold values from 1 to 12, as said below
- edge_dst: int32 [8, 4, 2, 12, 256], P(('pipe', 'row'), 'rep'), may hold values from 0 to 63
- edge_src: int32 [8, 4, 2, 12, 256], P(('pipe', 'row'), 'rep'), may hold values from 0 to 63
- edge_weight: float32 [8, 4, 2, 12, 256], P(('pipe', 'row'), 'rep'), may hold values from 0.25 to 4
- w_msg: bfloat16 [2, 256, 256], replicated, may hold values from -0.375 to 0.375
- w_self: bfloat16 [2, 256, 256], replicated, may hold values from -0.375 to 0.375
- w_mid: bfloat16 [2, 256, 256], replicated, may hold values from -0.375 to 0.375
- w_out: bfloat16 [2, 256, 256], replicated, may hold values from -0.375 to 0.375
- gain: float32 [2, 256], replicated, may hold values from 0.1 to 1.9
Outputs:
- hidden: bfloat16 [2, 1, 4096, 256], P(None, None, ('pipe', 'row'))
Inputs may be any that keep to these rules, and one draw needn't show every extreme that they name: `tile_count`: every entry is at least 1 and at most 12; for every row block and every index of rep, some section has exactly 12 live slots.
All inputs are finite; a program needn't handle non-finite values.
Results may differ from a plain program's by a relative error of at most 0.0054.
Values may be sent and summed in bfloat16 or wider, within the bound.
A program may use at most 64 MiB of HBM per device.

v0:
```python
import jax
import jax.numpy as jnp
from jax import lax
from jax.sharding import PartitionSpec as P

BS = 64
LAYERS = 2


def build_tiles(dst, src, weight):
    hot_dst = (dst[..., None] == jnp.arange(BS)).astype(jnp.float32) * weight[..., None]
    hot_src = (src[..., None] == jnp.arange(BS)).astype(jnp.float32)
    made = jnp.einsum("...ea,...eb->...ab", hot_dst, hot_src, precision=lax.Precision.HIGHEST)
    return made.astype(jnp.bfloat16)


def section_product(source, tiles_now, src_now, hot_now):
    rows, width = source.shape
    blocked = source.reshape(rows // BS, BS, width)
    picked = jnp.take(blocked, src_now, axis=0)
    prod = jnp.einsum("kab,kbf->kaf", tiles_now, picked, preferred_element_type=jnp.float32)
    summed = jnp.einsum("kn,kaf->naf", hot_now, prod, precision=lax.Precision.HIGHEST)
    return summed.reshape(rows, width)


def update_rows(rows_in, summed, wself, wmid, wout, gain_row):
    stat = jnp.mean(summed * summed, axis=-1, keepdims=True)
    normed = summed * lax.rsqrt(stat + 1e-05) * gain_row
    pre = jnp.dot(rows_in, wself, preferred_element_type=jnp.float32) + normed
    first = jax.nn.silu(pre).astype(jnp.bfloat16)
    second = jax.nn.silu(jnp.dot(first, wmid, preferred_element_type=jnp.float32)).astype(
        jnp.bfloat16
    )
    return (
        rows_in.astype(jnp.float32) + jnp.dot(second, wout, preferred_element_type=jnp.float32)
    ).astype(jnp.bfloat16)


def on_device(
    features,
    tile_src,
    tile_dst,
    tile_count,
    edge_dst,
    edge_src,
    edge_weight,
    w_msg,
    w_self,
    w_mid,
    w_out,
    gain,
):
    events, rows, width = features.shape
    blocks = rows // BS
    slots = tile_src.shape[3]
    rep_count = lax.axis_size("rep")
    my_rep = lax.axis_index("rep")
    quarter = width // rep_count
    tiles = build_tiles(edge_dst[0, 0], edge_src[0, 0], edge_weight[0, 0])
    live_int = (jnp.arange(slots)[None, :] < tile_count[0, 0][:, None]).astype(jnp.int32)
    src_idx = tile_src[0, 0]
    dst_idx = tile_dst[0, 0]
    tiles_all = lax.all_gather(tiles[None], "rep", axis=0, tiled=True)
    index_all = lax.all_gather(
        jnp.stack([src_idx, dst_idx, live_int])[None], "rep", axis=0, tiled=True
    )
    results = []
    for level in range(LAYERS):
        results.append([])
    state = features[0]
    for level in range(LAYERS):
        wmsg = w_msg[level]
        wself = w_self[level]
        wmid = w_mid[level]
        wout = w_out[level]
        gain_row = gain[level]
        y = jnp.dot(state, wmsg, preferred_element_type=jnp.float32).astype(jnp.bfloat16)
        y_share = lax.dynamic_slice_in_dim(y, my_rep * quarter, quarter, 1)
        piece = lax.all_gather(y_share, ("pipe", "row"), axis=0, tiled=True)
        count = piece.shape[0] // rows

        def one_block(i, acc):
            owner_rep = i % rep_count
            section = i // rep_count
            tiles_rep = lax.dynamic_index_in_dim(tiles_all, owner_rep, 0, keepdims=False)
            tiles_now = lax.dynamic_index_in_dim(tiles_rep, section, 0, keepdims=False)
            info_rep = lax.dynamic_index_in_dim(index_all, owner_rep, 0, keepdims=False)
            info = lax.dynamic_index_in_dim(info_rep, section, 1, keepdims=False)
            hot_now = (info[1][:, None] == jnp.arange(blocks)).astype(jnp.float32) * info[2].astype(
                jnp.float32
            )[:, None]
            sub = lax.dynamic_slice_in_dim(piece, i * rows, rows, 0)
            return acc + section_product(sub, tiles_now, info[0], hot_now)

        column_sum = lax.fori_loop(0, count, one_block, jnp.zeros((rows, quarter), jnp.float32))
        summed = lax.all_gather(column_sum, "rep", axis=1, tiled=True)
        state = update_rows(state, summed, wself, wmid, wout, gain_row)
        results[level].append(state)
    return jnp.stack([jnp.stack(items) for items in results])


def solution(mesh):
    placed = (
        P(None, ("pipe", "row"), None),
        P(("pipe", "row"), "rep", None, None),
        P(("pipe", "row"), "rep", None, None),
        P(("pipe", "row"), "rep", None),
        P(("pipe", "row"), "rep", None, None, None),
        P(("pipe", "row"), "rep", None, None, None),
        P(("pipe", "row"), "rep", None, None, None),
        P(),
        P(),
        P(),
        P(),
        P(),
    )
    return jax.shard_map(
        on_device,
        mesh=mesh,
        in_specs=placed,
        out_specs=P(None, None, ("pipe", "row"), None),
        check_vma=False,
    )
```

profile of v0, /device:TPU:0, one launch (start us, length us, event | category | flops | bytes accessed | tf_op | source)
XLA Modules:
  0.0 140.6 jit_solution(12819187617356729768)
XLA Ops:
  0.0 1.2 fusion.56
  1.3 27.9 %all_gather.20 = bf16[4096,64]{0,1:T(8,128)(2,1)S(1)} all-gather(bf16[512,64]{0,1:T(8,128)(2,1)S(1)} %dynamic-slice_convert_fusion.1), channel_id=1, replica_groups=mesh['pipe'=2,'row'=4,'rep'=4] {'pipe','row'}, dimensions={0}, use_global_device_ids=true | all-gather | bytes 589824 | tf_op jit(solution)/shard_map/all_gather | solution.py:79
  29.2 0.7 copy.31
  29.9 0.7 copy.32
  30.6 0.7 copy.33
  31.4 1.2 fusion.40
  32.6 18.9 %all-gather.1 = bf16[8,12,64,64]{3,2,1,0:T(8,128)(2,1)S(1)} all-gather(bf16[2,12,64,64]{3,2,1,0:T(8,128)(2,1)S(1)} %fusion.40), channel_id=3, replica_groups=mesh['pipe'=2,'row'=4,'rep'=4] {'rep'}, dimensions={0}, use_global_device_ids=true | all-gather | bytes 983040 | tf_op jit(solution)/shard_map/all_gather | solution.py:63
  51.6 8.3 %all-gather = s32[12,2,12]{2,1,0:T(2,128)S(1)} all-gather(s32[3,2,12]{2,1,0:T(2,128)S(1)} %pad_add_fusion), channel_id=2, replica_groups=mesh['pipe'=2,'row'=4,'rep'=4] {'rep'}, dimensions={0}, use_global_device_ids=true | all-gather | bytes 1440 | tf_op jit(solution)/shard_map/all_gather | solution.py:64
  59.9 15.6 %while.34 = (s32[]{:T(128)}, f32[512,64]{0,1:T(8,128)S(1)}, s32[4,3,2,12]{3,2,1,0:T(2,128)S(1)}, bf16[4,2,12,64,64]{4,3,2,1,0:T(8,128)(2,1)S(1)}, bf16[4096,64]{...) while((s32[]{:T(128)}, f32[512,64]{0,1:T(8,128)S(1)}, ...), condition=%wide.region_1.3_spmd.clone, body=%wide.region_0.2_spmd.clone.sunk | while | flops 11126065 | bytes 2430404 | solution.py:95
  60.1 0.6 gather_fusion
  61.3 0.4 fusion.117
  62.1 0.6 gather_fusion
  63.2 0.4 fusion.117
  64.0 0.6 gather_fusion
  65.2 0.4 fusion.117
  66.0 0.6 gather_fusion
  67.2 0.4 fusion.117
  67.9 0.6 gather_fusion
  69.1 0.4 fusion.117
  69.9 0.6 gather_fusion
  71.1 0.4 fusion.117
  71.8 0.6 gather_fusion
  73.0 0.4 fusion.117
  73.8 0.6 gather_fusion
  75.0 0.4 fusion.117
  75.6 9.3 %all_gather.21 = f32[512,256]{0,1:T(8,128)S(1)} all-gather(f32[512,64]{0,1:T(8,128)S(1)} %get-tuple-element.330), channel_id=1, replica_groups=mesh['pipe'=2,'row'=4,'rep'=4] {'rep'}, dimensions={1}, use_global_device_ids=true | all-gather | bytes 655360 | tf_op jit(solution)/shard_map/all_gather | solution.py:96
  85.2 1.4 multiply_convert_fusion.2
  87.2 26.4 %all_gather.22 = bf16[4096,64]{0,1:T(8,128)(2,1)S(1)} all-gather(bf16[512,64]{0,1:T(8,128)(2,1)S(1)} %dynamic-slice_convert_fusion), channel_id=1, replica_groups=mesh['pipe'=2,'row'=4,'rep'=4] {'pipe','row'}, dimensions={0}, use_global_device_ids=true | all-gather | bytes 589824 | tf_op jit(solution)/shard_map/all_gather | solution.py:79
  113.6 15.5 %while.35 = (s32[]{:T(128)}, f32[512,64]{0,1:T(8,128)S(1)}, s32[4,3,2,12]{3,2,1,0:T(2,128)S(1)}, bf16[4,2,12,64,64]{4,3,2,1,0:T(8,128)(2,1)S(1)}, bf16[4096,64]{...) while((s32[]{:T(128)}, f32[512,64]{0,1:T(8,128)S(1)}, ...), condition=%wide.region_4.6_spmd.clone, body=%wide.region_3.5_spmd.clone.sunk | while | flops 11126065 | bytes 2430404 | solution.py:95
  113.8 0.6 gather_fusion.1
  115.0 0.4 fusion.124
  115.7 0.6 gather_fusion.1
  116.9 0.4 fusion.124
  117.7 0.6 gather_fusion.1
  118.8 0.4 fusion.124
  119.6 0.6 gather_fusion.1
  121.6 0.6 gather_fusion.1
  122.7 0.4 fusion.124
  123.5 0.6 gather_fusion.1
  124.7 0.4 fusion.124
  125.5 0.6 gather_fusion.1
  126.6 0.4 fusion.124
  127.4 0.6 gather_fusion.1
  128.6 0.4 fusion.124
  129.2 9.1 %all_gather.23 = f32[512,256]{0,1:T(8,128)S(1)} all-gather(f32[512,64]{0,1:T(8,128)S(1)} %get-tuple-element.331), channel_id=1, replica_groups=mesh['pipe'=2,'row'=4,'rep'=4] {'rep'}, dimensions={1}, use_global_device_ids=true | all-gather | bytes 655360 | tf_op jit(solution)/shard_map/all_gather | solution.py:96
  138.6 0.4 multiply_convert_fusion
  139.0 0.5 copy-done.3
  139.8 0.8 pad_maximum_fusion
  (182 shorter events, 15.6 us)
Async XLA Ops:
  31.4 20.1 %copy-start.10 = (s32[1,1,2]{2,1,0:T(1,128)S(1)}, s32[1,1,2]{2,1,0:T(1,128)}, u32[]{:S(2)}) copy-start(s32[1,1,2]{2,1,0:T(1,128)} %param.21) | copy-start | bytes 28
  31.4 20.2 %copy-start.5 = (s32[1,1,2,12]{3,2,1,0:T(2,128)S(1)}, s32[1,1,2,12]{3,2,1,0:T(2,128)}, u32[]{:S(2)}) copy-start(s32[1,1,2,12]{3,2,1,0:T(2,128)} %param.20) | copy-start | bytes 292
  31.4 20.2 %copy-start.6 = (s32[1,1,2,12]{3,2,1,0:T(2,128)S(1)}, s32[1,1,2,12]{3,2,1,0:T(2,128)}, u32[]{:S(2)}) copy-start(s32[1,1,2,12]{3,2,1,0:T(2,128)} %param.19) | copy-start | bytes 292
  75.5 9.6 %copy-start.4 = (f32[2,256]{1,0:T(2,128)S(1)}, f32[2,256]{1,0:T(2,128)}, u32[]{:S(2)}) copy-start(f32[2,256]{1,0:T(2,128)} %param.29) | copy-start | bytes 6148
  75.5 9.6 %copy-start = (bf16[1,512,256]{2,1,0:T(8,128)(2,1)S(1)}, bf16[1,512,256]{2,1,0:T(8,128)(2,1)}, u32[]{:S(2)}) copy-start(bf16[1,512,256]{2,1,0:T(8,128)(2,1)} %param.18) | copy-start | bytes 786436
  75.6 9.6 %copy-start.7 = (bf16[2,256,256]{2,1,0:T(8,128)(2,1)S(1)}, bf16[2,256,256]{2,1,0:T(8,128)(2,1)}, u32[]{:S(2)}) copy-start(bf16[2,256,256]{2,1,0:T(8,128)(2,1)} %param.27) | copy-start | bytes 786436
  85.2 1.4 %copy-start.2 = (bf16[2,256,256]{2,1,0:T(8,128)(2,1)S(1)}, bf16[2,256,256]{2,1,0:T(8,128)(2,1)}, u32[]{:S(2)}) copy-start(bf16[2,256,256]{2,1,0:T(8,128)(2,1)} %param.28) | copy-start | bytes 786436
  85.2 1.7 %copy-start.1 = (bf16[2,256,256]{2,1,0:T(8,128)(2,1)S(1)}, bf16[2,256,256]{2,1,0:T(8,128)(2,1)}, u32[]{:S(2)}) copy-start(bf16[2,256,256]{2,1,0:T(8,128)(2,1)} %param.25) | copy-start | bytes 786436
  129.1 9.4 %copy-start.8 = (bf16[2,256,256]{2,1,0:T(8,128)(2,1)S(1)}, bf16[2,256,256]{2,1,0:T(8,128)(2,1)}, u32[]{:S(2)}) copy-start(bf16[2,256,256]{2,1,0:T(8,128)(2,1)} %param.27) | copy-start | bytes 786436
  129.1 9.4 %copy-start.9 = (bf16[2,256,256]{2,1,0:T(8,128)(2,1)S(1)}, bf16[2,256,256]{2,1,0:T(8,128)(2,1)}, u32[]{:S(2)}) copy-start(bf16[2,256,256]{2,1,0:T(8,128)(2,1)} %param.26) | copy-start | bytes 786436
  138.6 1.0 copy-start.3
where the time goes:
time: 141 us
  blocking collectives  100 us (71%)
  local copies, waits for them, and re-layouts  20.9 us (15%)
  matrix products  15.4 us (11%)
  other arithmetic  2.33 us (2%)
  loops' own time  1.8 us (1%)
    all_gather x2, blocking collectives, on_device(): piece = lax.all_gather(y_share, ('pipe', 'row'), axis=0, tiled=True)  54.3 us
    all_gather x1, blocking collectives, on_device(): tiles_all = lax.all_gather(tiles[None], 'rep', axis=0, tiled=True)  18.9 us
    all_gather x2, blocking collectives, on_device(): summed = lax.all_gather(column_sum, 'rep', axis=1, tiled=True)  18.4 us
    gather x16, local copies, waits for them, and re-layouts, section_product(): picked = jnp.take(blocked, src_now, axis=0)  9.42 us
    all_gather x1, blocking collectives, on_device(): lax.all_gather(jnp.stack([src_idx, dst_idx, live_int])[None], 'rep', axis...  8.33 us
    dot_general x16, matrix products, section_product(): jnp.einsum('kn,kaf->naf', hot_now, prod, precision=lax.Precision.HIGHEST)  6.06 us
    dot_general x16, local copies, waits for them, and re-layouts, section_product(): jnp.einsum('kab,kbf->kaf', tiles_now, picked, preferred_element_type=jnp....  4.37 us
    dot_general x16, matrix products, section_product(): jnp.einsum('kab,kbf->kaf', tiles_now, picked, preferred_element_type=jnp....  4.28 us

commit v1 on v0

--- a/solution.py
+++ b/solution.py
@@ -5,6 +5,18 @@
 
 BS = 64
 LAYERS = 2
+
+
+def collect(x, axis, dim):
+    ways, here = (lax.axis_size(axis), lax.axis_index(axis))
+    grown, reach = (x, 1)
+    while reach < ways:
+        theirs = lax.ppermute(grown, axis, [(d, d ^ reach) for d in range(ways)])
+        mine_first = jnp.concatenate([grown, theirs], axis=dim)
+        theirs_first = jnp.concatenate([theirs, grown], axis=dim)
+        grown = jnp.where(here & reach == 0, mine_first, theirs_first)
+        reach = 2 * reach
+    return grown
 
 
 def build_tiles(dst, src, weight):
@@ -76,7 +88,7 @@
         gain_row = gain[level]
         y = jnp.dot(state, wmsg, preferred_element_type=jnp.float32).astype(jnp.bfloat16)
         y_share = lax.dynamic_slice_in_dim(y, my_rep * quarter, quarter, 1)
-        piece = lax.all_gather(y_share, ("pipe", "row"), axis=0, tiled=True)
+        piece = collect(y_share, ("pipe", "row"), 0)
         count = piece.shape[0] // rows
 
         def one_block(i, acc):

time: 141 us -> 105 us (0.74)
  blocking collectives: 100 us -> 44.5 us
  waiting for transfers between devices: 0 us -> 12.1 us
  starting transfers between devices: 0 us -> 7.08 us
    all_gather x2 -> x0, blocking collectives: 54.3 us -> none  [on_device(): piece = lax.all_gather(y_share, ('pipe', 'row'), axis=0, tiled=True)]
    ppermute x0 -> x6, waiting for transfers between devices: none -> 12.1 us  [collect(): theirs = lax.ppermute(grown, axis, [(d, d ^ reach) for d in range(ways)])]
    ppermute x0 -> x6, starting transfers between devices: none -> 7.08 us  [collect(): theirs = lax.ppermute(grown, axis, [(d, d ^ reach) for d in range(ways)])]
    all_gather x1, blocking collectives: 18.9 us -> 16.8 us  [on_device(): tiles_all = lax.all_gather(tiles[None], 'rep', axis=0, tiled=True)]
  transfers between devices with their start and end apart: 0 -> 6, of which waited for: 0 -> 3; matrix products, arithmetic and copies ran while one was open for 0% -> 3% of each run, Pallas kernels for 0% -> 0%
where the time goes in v1:
time: 105 us
  blocking collectives  44.5 us (42%)
  local copies, waits for them, and re-layouts  20.9 us (20%)
  matrix products  15.4 us (15%)
  waiting for transfers between devices  12.1 us (12%)
  starting transfers between devices  7.08 us (7%)
  other arithmetic  2.8 us (3%)
  loops' own time  1.86 us (2%)
    all_gather x2, blocking collectives, on_device(): summed = lax.all_gather(column_sum, 'rep', axis=1, tiled=True)  19.7 us
    all_gather x1, blocking collectives, on_device(): tiles_all = lax.all_gather(tiles[None], 'rep', axis=0, tiled=True)  16.8 us
    ppermute x6, waiting for transfers between devices, collect(): theirs = lax.ppermute(grown, axis, [(d, d ^ reach) for d in range(ways)])  12.1 us
    gather x16, local copies, waits for them, and re-layouts, section_product(): picked = jnp.take(blocked, src_now, axis=0)  9.41 us
    all_gather x1, blocking collectives, on_device(): lax.all_gather(jnp.stack([src_idx, dst_idx, live_int])[None], 'rep', axis...  7.95 us
    ppermute x6, starting transfers between devices, collect(): theirs = lax.ppermute(grown, axis, [(d, d ^ reach) for d in range(ways)])  7.08 us
    dot_general x16, matrix products, section_product(): jnp.einsum('kn,kaf->naf', hot_now, prod, precision=lax.Precision.HIGHEST)  6.05 us
    dot_general x16, local copies, waits for them, and re-layouts, section_product(): jnp.einsum('kab,kbf->kaf', tiles_now, picked, preferred_element_type=jnp....  4.37 us
  transfers between devices with their start and end apart: 6, of which 3 were waited for; matrix products, arithmetic and copies ran while one was open for 3% of the time, Pallas kernels for 0%

profile of v1, /device:TPU:0, one launch (start us, length us, event | category | flops | bytes accessed | tf_op | source)
XLA Modules:
  0.0 105.0 jit_solution(17615854771820416448)
XLA Ops:
  0.0 1.3 %fusion.56 = bf16[512,256]{0,1:T(8,128)(2,1)S(1)} fusion(bf16[1,512,256]{2,1,0:T(8,128)(2,1)} %param.18, bf16[2,256,256]{2,1,0:T(8,128)(2,1)} %param.25), kind=kOutput, calls=%fused_computation.91 | convolution fusion | flops 67108864 | bytes 655360 | tf_op jit(solution)/shard_map/dot_general | solution.py:89
  1.3 3.1 %collective-permute-start = (bf16[512,64]{0,1:T(8,128)(2,1)S(1)}, bf16[512,64]{0,1:T(8,128)(2,1)S(1)}, u32[]{:S(2)}, u32[]{:S(2)}) collective-permute-start(bf16[512,64]{0,1:T(8,128)(2,1)S(1)} %dynamic-slice_convert_fusion.1), channel_id=1, source_target_pairs={{0,4},{4,0},{8,12},{12,8},{16,20},{20,16},{24,28},{28,24},{1,5},{5... | collective-permute-start | bytes 196616 | tf_op jit(solution)/shard_map/ppermute | solution.py:14
  4.4 0.7 copy.31
  5.2 0.7 copy.32
  5.9 0.7 copy.33
  6.6 1.2 %fusion.40 = bf16[2,12,64,64]{3,2,1,0:T(8,128)(2,1)S(1)} fusion(s32[2,12,256]{2,1,0:T(8,128)S(1)} %copy.33, f32[2,12,256]{2,1,0:T(8,128)S(1)} %copy.32, s32[2,12,256]{2,1,0:T(8,128)S(1)} %copy.31), kind=kOutput, calls=%fused_computation.62 | convolution fusion | flops 303267840 | bytes 270336 | tf_op jit(solution)/shard_map/...ea,...eb->...ab/dot_general | solution.py:25
  8.0 2.7 %collective-permute-start.1 = (bf16[1024,64]{0,1:T(8,128)(2,1)S(1)}, bf16[1024,64]{0,1:T(8,128)(2,1)S(1)}, u32[]{:S(2)}, u32[]{:S(2)}) collective-permute-start(bf16[1024,64]{0,1:T(8,128)(2,1)S(1)} %maximum_select_fusion.4), channel_id=1, source_target_pairs={{0,8},{4,12},{8,0},{12,4},{16,24},{20,28},{24,16},{28,20},{1,9},{5... | collective-permute-start | bytes 393224 | tf_op jit(solution)/shard_map/ppermute | solution.py:14
  10.7 16.8 %all-gather.1 = bf16[8,12,64,64]{3,2,1,0:T(8,128)(2,1)S(1)} all-gather(bf16[2,12,64,64]{3,2,1,0:T(8,128)(2,1)S(1)} %fusion.40), channel_id=3, replica_groups=mesh['pipe'=2,'row'=4,'rep'=4] {'rep'}, dimensions={0}, use_global_device_ids=true | all-gather | bytes 983040 | tf_op jit(solution)/shard_map/all_gather | solution.py:75
  27.7 8.0 %all-gather = s32[12,2,12]{2,1,0:T(2,128)S(1)} all-gather(s32[3,2,12]{2,1,0:T(2,128)S(1)} %pad_add_fusion), channel_id=2, replica_groups=mesh['pipe'=2,'row'=4,'rep'=4] {'rep'}, dimensions={0}, use_global_device_ids=true | all-gather | bytes 1440 | tf_op jit(solution)/shard_map/all_gather | solution.py:76
  35.8 15.6 %while.34 = (s32[]{:T(128)}, f32[512,64]{0,1:T(8,128)S(1)}, s32[4,3,2,12]{3,2,1,0:T(2,128)S(1)}, bf16[4,2,12,64,64]{4,3,2,1,0:T(8,128)(2,1)S(1)}, bf16[4096,64]{...) while((s32[]{:T(128)}, f32[512,64]{0,1:T(8,128)S(1)}, ...), condition=%wide.region_1.3_spmd.clone, body=%wide.region_0.2_spmd.clone.sunk | while | flops 11126065 | bytes 2430404 | solution.py:107
  36.0 0.6 gather_fusion
  37.9 0.6 gather_fusion
  39.1 0.4 fusion.117
  39.9 0.6 gather_fusion
  41.8 0.6 gather_fusion
  43.0 0.4 fusion.117
  43.8 0.6 gather_fusion
  44.9 0.4 fusion.117
  45.7 0.6 gather_fusion
  46.9 0.4 fusion.117
  47.7 0.6 gather_fusion
  48.8 0.4 fusion.117
  49.6 0.6 gather_fusion
  50.8 0.4 fusion.117
  51.3 9.9 %all_gather.14 = f32[512,256]{0,1:T(8,128)S(1)} all-gather(f32[512,64]{0,1:T(8,128)S(1)} %get-tuple-element.330), channel_id=1, replica_groups=mesh['pipe'=2,'row'=4,'rep'=4] {'rep'}, dimensions={1}, use_global_device_ids=true | all-gather | bytes 655360 | tf_op jit(solution)/shard_map/all_gather | solution.py:108
  61.6 1.5 %multiply_convert_fusion.2 = bf16[512,256]{1,0:T(8,128)(2,1)S(1)} fusion(f32[512,256]{1,0:T(8,128)S(1)} %copy.35, bf16[1,512,256]{2,1,0:T(8,128)(2,1)S(1)} %copy-done, f32[256]{0:T(256)S(1)} %bitcast.119, f32[512]{0:T(512)S(1)} %add_rsqrt_fusion.1, bf16[2,256,256]{2,1,0:T(8,128)(2,1)} %param.27, bf16[2,256,256]{2,1,0:T(8,128)(2,1)} %param.26), kind=kOutput, calls=%fused_computation.83 | convolution fusion | flops 135921664 | bytes 1313792 | tf_op jit(solution)/shard_map/dot_general | solution.py:43
  63.6 0.7 collective-permute-start.3
  64.3 4.3 %collective-permute-done.3 = bf16[512,64]{0,1:T(8,128)(2,1)S(1)} collective-permute-done((bf16[512,64]{0,1:T(8,128)(2,1)S(1)}, bf16[512,64]{0,1:T(8,128)(2,1)S(1)}, u32[]{:S(2)}, u32[]{:S(2)}) %collective-permute-start.3) | collective-permute-done | bytes 65568 | tf_op jit(solution)/shard_map/ppermute | solution.py:14
  68.6 0.5 collective-permute-start.4
  69.1 6.3 %collective-permute-done.4 = bf16[1024,64]{0,1:T(8,128)(2,1)S(1)} collective-permute-done((bf16[1024,64]{0,1:T(8,128)(2,1)S(1)}, bf16[1024,64]{0,1:T(8,128)(2,1)S(1)}, u32[]{:S(2)}, u32[]{:S(2)}) %collective-permute-start.4) | collective-permute-done | bytes 131104 | tf_op jit(solution)/shard_map/ppermute | solution.py:14
  75.6 1.5 %collective-permute-done.5 = bf16[2048,64]{0,1:T(8,128)(2,1)S(1)} collective-permute-done((bf16[2048,64]{0,1:T(8,128)(2,1)S(1)}, bf16[2048,64]{0,1:T(8,128)(2,1)S(1)}, u32[]{:S(2)}, u32[]{:S(2)}) %collective-permute-start.5) | collective-permute-done | bytes 262176 | tf_op jit(solution)/shard_map/ppermute | solution.py:14
  77.2 15.6 %while.35 = (s32[]{:T(128)}, f32[512,64]{0,1:T(8,128)S(1)}, s32[4,3,2,12]{3,2,1,0:T(2,128)S(1)}, bf16[4,2,12,64,64]{4,3,2,1,0:T(8,128)(2,1)S(1)}, bf16[4096,64]{...) while((s32[]{:T(128)}, f32[512,64]{0,1:T(8,128)S(1)}, ...), condition=%wide.region_4.6_spmd.clone, body=%wide.region_3.5_spmd.clone.sunk | while | flops 11126065 | bytes 2430404 | solution.py:107
  77.4 0.6 gather_fusion.1
  79.4 0.6 gather_fusion.1
  81.3 0.6 gather_fusion.1
  82.5 0.4 fusion.124
  83.3 0.6 gather_fusion.1
  84.5 0.4 fusion.124
  85.2 0.6 gather_fusion.1
  86.4 0.4 fusion.124
  87.2 0.6 gather_fusion.1
  88.4 0.4 fusion.124
  89.1 0.6 gather_fusion.1
  91.1 0.6 gather_fusion.1
  92.9 9.8 %all_gather.15 = f32[512,256]{0,1:T(8,128)S(1)} all-gather(f32[512,64]{0,1:T(8,128)S(1)} %get-tuple-element.331), channel_id=1, replica_groups=mesh['pipe'=2,'row'=4,'rep'=4] {'rep'}, dimensions={1}, use_global_device_ids=true | all-gather | bytes 655360 | tf_op jit(solution)/shard_map/all_gather | solution.py:108
  103.0 0.4 multiply_convert_fusion
  103.4 0.5 copy-done.3
  104.1 0.8 pad_maximum_fusion
  (196 shorter events, 18.2 us)
Async XLA Ops:
  0.0 7.9 %copy-start.9 = (s32[1,1,2]{2,1,0:T(1,128)S(1)}, s32[1,1,2]{2,1,0:T(1,128)}, u32[]{:S(2)}) copy-start(s32[1,1,2]{2,1,0:T(1,128)} %param.21) | copy-start | bytes 28
  1.3 6.7 %collective-permute-start = (bf16[512,64]{0,1:T(8,128)(2,1)S(1)}, bf16[512,64]{0,1:T(8,128)(2,1)S(1)}, u32[]{:S(2)}, u32[]{:S(2)}) collective-permute-start(bf16[512,64]{0,1:T(8,128)(2,1)S(1)} %dynamic-slice_convert_fusion.1), channel_id=1, source_target_pairs={{0,4},{4,0},{8,12},{12,8},{16,20},{20,16},{24,28},{28,24},{1,5},{5... | collective-permute-start | bytes 196616 | tf_op jit(solution)/shard_map/ppermute | solution.py:14
  7.8 19.8 %copy-start.5 = (s32[1,1,2,12]{3,2,1,0:T(2,128)S(1)}, s32[1,1,2,12]{3,2,1,0:T(2,128)}, u32[]{:S(2)}) copy-start(s32[1,1,2,12]{3,2,1,0:T(2,128)} %param.20) | copy-start | bytes 292
  7.9 19.8 %copy-start.6 = (s32[1,1,2,12]{3,2,1,0:T(2,128)S(1)}, s32[1,1,2,12]{3,2,1,0:T(2,128)}, u32[]{:S(2)}) copy-start(s32[1,1,2,12]{3,2,1,0:T(2,128)} %param.19) | copy-start | bytes 292
  7.9 27.7 %copy-start.4 = (f32[2,256]{1,0:T(2,128)S(1)}, f32[2,256]{1,0:T(2,128)}, u32[]{:S(2)}) copy-start(f32[2,256]{1,0:T(2,128)} %param.29) | copy-start | bytes 6148
  8.0 19.4 %collective-permute-start.1 = (bf16[1024,64]{0,1:T(8,128)(2,1)S(1)}, bf16[1024,64]{0,1:T(8,128)(2,1)S(1)}, u32[]{:S(2)}, u32[]{:S(2)}) collective-permute-start(bf16[1024,64]{0,1:T(8,128)(2,1)S(1)} %maximum_select_fusion.4), channel_id=1, source_target_pairs={{0,8},{4,12},{8,0},{12,4},{16,24},{20,28},{24,16},{28,20},{1,9},{5... | collective-permute-start | bytes 393224 | tf_op jit(solution)/shard_map/ppermute | solution.py:14
  27.5 8.1 %collective-permute-start.2 = (bf16[2048,64]{0,1:T(8,128)(2,1)S(1)}, bf16[2048,64]{0,1:T(8,128)(2,1)S(1)}, u32[]{:S(2)}, u32[]{:S(2)}) collective-permute-start(bf16[2048,64]{0,1:T(8,128)(2,1)S(1)} %maximum_select_fusion.2), channel_id=1, source_target_pairs={{0,16},{4,20},{8,24},{12,28},{16,0},{20,4},{24,8},{28,12},{1,17},{... | collective-permute-start | bytes 786440 | tf_op jit(solution)/shard_map/ppermute | solution.py:14
  51.3 10.2 %copy-start = (bf16[1,512,256]{2,1,0:T(8,128)(2,1)S(1)}, bf16[1,512,256]{2,1,0:T(8,128)(2,1)}, u32[]{:S(2)}) copy-start(bf16[1,512,256]{2,1,0:T(8,128)(2,1)} %param.18) | copy-start | bytes 786436
  61.6 1.5 %copy-start.2 = (bf16[2,256,256]{2,1,0:T(8,128)(2,1)S(1)}, bf16[2,256,256]{2,1,0:T(8,128)(2,1)}, u32[]{:S(2)}) copy-start(bf16[2,256,256]{2,1,0:T(8,128)(2,1)} %param.28) | copy-start | bytes 786436
  61.6 1.7 %copy-start.1 = (bf16[2,256,256]{2,1,0:T(8,128)(2,1)S(1)}, bf16[2,256,256]{2,1,0:T(8,128)(2,1)}, u32[]{:S(2)}) copy-start(bf16[2,256,256]{2,1,0:T(8,128)(2,1)} %param.25) | copy-start | bytes 786436
  63.6 4.9 %collective-permute-start.3 = (bf16[512,64]{0,1:T(8,128)(2,1)S(1)}, bf16[512,64]{0,1:T(8,128)(2,1)S(1)}, u32[]{:S(2)}, u32[]{:S(2)}) collective-permute-start(bf16[512,64]{0,1:T(8,128)(2,1)S(1)} %dynamic-slice_convert_fusion), channel_id=1, source_target_pairs={{0,4},{4,0},{8,12},{12,8},{16,20},{20,16},{24,28},{28,24},{1,5},{5... | collective-permute-start | bytes 196616 | tf_op jit(solution)/shard_map/ppermute | solution.py:14
  68.6 6.8 %collective-permute-start.4 = (bf16[1024,64]{0,1:T(8,128)(2,1)S(1)}, bf16[1024,64]{0,1:T(8,128)(2,1)S(1)}, u32[]{:S(2)}, u32[]{:S(2)}) collective-permute-start(bf16[1024,64]{0,1:T(8,128)(2,1)S(1)} %maximum_select_fusion.5), channel_id=1, source_target_pairs={{0,8},{4,12},{8,0},{12,4},{16,24},{20,28},{24,16},{28,20},{1,9},{5... | collective-permute-start | bytes 393224 | tf_op jit(solution)/shard_map/ppermute | solution.py:14
  75.5 1.6 %collective-permute-start.5 = (bf16[2048,64]{0,1:T(8,128)(2,1)S(1)}, bf16[2048,64]{0,1:T(8,128)(2,1)S(1)}, u32[]{:S(2)}, u32[]{:S(2)}) collective-permute-start(bf16[2048,64]{0,1:T(8,128)(2,1)S(1)} %maximum_select_fusion.3), channel_id=1, source_target_pairs={{0,16},{4,20},{8,24},{12,28},{16,0},{20,4},{24,8},{28,12},{1,17},{... | collective-permute-start | bytes 786440 | tf_op jit(solution)/shard_map/ppermute | solution.py:14
  92.8 10.1 %copy-start.7 = (bf16[2,256,256]{2,1,0:T(8,128)(2,1)S(1)}, bf16[2,256,256]{2,1,0:T(8,128)(2,1)}, u32[]{:S(2)}) copy-start(bf16[2,256,256]{2,1,0:T(8,128)(2,1)} %param.27) | copy-start | bytes 786436
  92.8 10.1 %copy-start.8 = (bf16[2,256,256]{2,1,0:T(8,128)(2,1)S(1)}, bf16[2,256,256]{2,1,0:T(8,128)(2,1)}, u32[]{:S(2)}) copy-start(bf16[2,256,256]{2,1,0:T(8,128)(2,1)} %param.26) | copy-start | bytes 786436
  103.0 1.0 copy-start.3
